TPU v7x, 32 devices: a whole 2x2x4 slice. The times are simulated.
32 devices in a mesh: lat: 4 (over z), lon: 8 (over y, x, core).
Axes of the slice: x: 2, y: 2, z: 4, core: 2. Of those that a mesh axis runs over, the one named last changes fastest.
Arguments:
- covariance: float32 [4, 4, 128, 128], P('lat', None, 'lon'), may hold values from -6 to 6
- winds: float32 [2, 3, 4, 128], P(None, None, None, 'lon'), may hold values from -0.35 to 0.35
- diffusivity: float32 [4, 128], P(None, 'lon'), may hold values from 0.01 to 0.07
- cutoff: int32 [4], replicated, may hold values from 0 to 1, as said below
Outputs:
- forecast: float32 [4, 4, 128, 128], P('lat', None, 'lon')
Inputs may be any that keep to these rules, and one draw needn't show every extreme that they name: Some latitude has cutoff 1 and some other has 0.
All inputs are finite; a program needn't handle non-finite values.
Results may differ from a plain program's by a relative error of at most 0.00002.
Values sent between devices are 32-bit elements; how exact they have to be, the bound alone decides.
No kernel may reach another device: no remote copies, remote signals or barrier semaphores. Data moves between devices by JAX's collectives and lax.ppermute only.
A program may use at most 192 MiB of HBM per device.

v0:
```python
import functools

import jax
import jax.numpy as jnp
from jax import lax
from jax.experimental import pallas as pl
from jax.experimental.pallas import tpu as pltpu
from jax.sharding import PartitionSpec as P

STEPS = 3
FIELDS = 2 * STEPS + 1
ROUTES = (
    (8, 9, 10, 11, 12, 13, 22, 14, 16, 17, 2, 27, 20, 21, 19, 31, 24, 25, 26, 23, 4, 5, 30, 7, 0, 1, 18, 3, 29, 28, 6, 15),
    (3, 17, 10, 19, 20, 29, 14, 23, 9, 25, 11, 15, 8, 12, 30, 6, 0, 1, 16, 27, 28, 13, 18, 22, 21, 24, 2, 26, 4, 5, 31, 7),
    (24, 25, 26, 27, 28, 21, 30, 15, 0, 1, 18, 19, 4, 5, 22, 7, 8, 20, 2, 3, 17, 29, 6, 31, 16, 9, 10, 11, 12, 13, 14, 23),
    (16, 0, 18, 2, 5, 4, 7, 31, 24, 1, 26, 3, 28, 29, 6, 23, 25, 9, 10, 11, 12, 13, 14, 15, 8, 17, 27, 19, 20, 21, 22, 30),
)
EXCHANGES = len(ROUTES)
VMEM = pl.BlockSpec(memory_space=pltpu.VMEM)


def shifted(shard, axis, by, wrap):
    size = lax.axis_size(axis)
    pairs = [(i, (i + by) % size) for i in range(size) if wrap or 0 <= i + by < size]
    return lax.ppermute(shard, axis, pairs)


def weights(east_wind, north_wind, spread):
    west = jnp.maximum(east_wind, 0.0) + spread
    east = spread - jnp.minimum(east_wind, 0.0)
    south = jnp.maximum(north_wind, 0.0) + spread
    north = spread - jnp.minimum(north_wind, 0.0)
    return west, east, south, north, 1.0 - (west + east + south + north)


def general(covariance, winds, diffusivity, cutoff):
    row_count, lat_count, lon_local, _ = covariance.shape
    blocks = lat_count // row_count
    device_index = lax.axis_index("lat")
    rows = device_index * row_count + jnp.arange(row_count, dtype=jnp.int32)
    lats = jnp.arange(lat_count, dtype=jnp.int32)
    keep = jnp.abs(lats[None, :] - rows[:, None]) <= cutoff[None, :]
    keep = keep[:, :, None, None]
    stacked = jnp.concatenate([winds.reshape(2 * STEPS, lat_count, lon_local), diffusivity[None]])
    everywhere = lax.all_gather(stacked, "lon", axis=2, tiled=True)
    left = shifted(stacked[:, :, -STEPS:], "lon", 1, True)
    right = shifted(stacked[:, :, :STEPS], "lon", -1, True)
    near = jnp.concatenate([left, stacked, right], axis=2)

    field = jnp.where(keep, covariance, 0.0)
    left = shifted(field[:, :, -STEPS:], "lon", 1, True)
    right = shifted(field[:, :, :STEPS], "lon", -1, True)
    field = jnp.concatenate([left, field, right], axis=2)
    for step in range(STEPS):
        width = near.shape[2] - 2 * step
        take = functools.partial(lax.slice_in_dim, start_index=step + 1, limit_index=step + width - 1, axis=1)
        west, east, south, north, own = (
            w[None, :, :, None]
            for w in weights(take(near[step]), take(near[STEPS + step]), take(near[2 * STEPS]))
        )
        center = field[:, :, 1:-1]
        none = jnp.zeros_like(center[:, :1])
        field = (
            own * center
            + west * field[:, :, :-2]
            + east * field[:, :, 2:]
            + south * jnp.concatenate([none, center[:, :-1]], axis=1)
            + north * jnp.concatenate([center[:, 1:], none], axis=1)
        )

    reach = min(-(-STEPS // row_count), blocks - 1)
    halo = min(STEPS, reach * row_count)
    below = [shifted(field, "lat", by, False) for by in range(reach, 0, -1)]
    above = [shifted(field, "lat", -by, False) for by in range(1, reach + 1)]
    window = jnp.concatenate([*below, field, *above])
    window = window[reach * row_count - halo : (reach + 1) * row_count + halo]
    padded = jnp.pad(everywhere, ((0, 0), (halo, halo), (0, 0)))
    local = lax.dynamic_slice_in_dim(padded, device_index * row_count, row_count + 2 * halo, 1)
    for step in range(STEPS):
        west, east, south, north, own = (
            w[:, None, None, :] for w in weights(local[step], local[STEPS + step], local[2 * STEPS])
        )
        none = jnp.zeros_like(window[:1])
        window = (
            own * window
            + west * jnp.roll(window, 1, axis=3)
            + east * jnp.roll(window, -1, axis=3)
            + south * jnp.concatenate([none, window[:-1]])
            + north * jnp.concatenate([window[1:], none])
        )
        inside = device_index * row_count - halo + jnp.arange(window.shape[0])
        inside = (inside >= 0) & (inside < lat_count)
        window = jnp.where(inside[:, None, None, None], window, 0.0)
    return jnp.where(keep, window[halo : halo + row_count], 0.0)


def place():
    lon = lax.axis_index("lon")
    return lax.axis_index("lat"), lon, lax.rem(lon, 2)


def packed_rows(at, coming, first, blocks):
    route, rows, word = ROUTES[at], 4, 0
    for block in range(first, first + 4):
        for row in range(rows):
            device = blocks * row + block
            other = route.index(device) if coming else route[device]
            same = other % blocks == block
            word |= (other // blocks if same else row) << 2 * (rows * (block - first) + row)
    return jnp.int32(word - (1 << 32) if word >> 31 else word)


def rows_here(coming):
    lat, lon, _ = place()
    blocks = lax.axis_size("lon")
    at = 2 * (4 * (lon & 3) + lat)
    words = [
        jnp.where(lon < 4, *(packed_rows(step, coming, first, blocks) for first in (0, 4)))
        for step in range(EXCHANGES)
    ]
    return [lax.shift_right_logical(word, at) & 3 for word in words]


def prepare_kernel(
    cutoff_in,
    covariance_in,
    winds_in,
    diffusivity_in,
    to_core,
    to_cross,
    packed,
    banded,
    kept,
    cutoff,
    covariance,
    winds,
    diffusivity,
    arrived,
):
    copies = [
        pltpu.make_async_copy(source, target, arrived.at[at])
        for at, (source, target) in enumerate(
            (
                (winds_in, winds),
                (diffusivity_in, diffusivity),
                (covariance_in, covariance),
                (cutoff_in, cutoff),
            )
        )
    ]
    for copy in copies:
        copy.start()
    lat, _, core = place()
    lats, width, lon_count = banded.shape
    packed[...] = jnp.zeros_like(packed)
    copies[0].wait()
    copies[1].wait()
    for step in range(STEPS):
        for kind in range(2):
            at = (kind * STEPS + step) * width
            packed[:, at : at + width] = winds[kind, step]
    packed[:, 2 * STEPS * width : FIELDS * width] = diffusivity[...]
    rows = pl.ds(lats * STEPS, lats)
    to_core[rows] = packed[...]
    to_cross[rows] = packed[...]
    copies[2].wait()
    copies[3].wait()
    for i in range(lats):
        keep = jnp.abs(i - lat) <= cutoff[i]
        kept[i : i + 1] = jnp.full((1, lon_count), jnp.where(keep, 1.0, 0.0), jnp.float32)
        banded[i] = jnp.where(keep, covariance[0, i], 0.0)
        first, last = banded[i, :STEPS], banded[i, width - STEPS :]
        rows = pl.ds(i * STEPS, STEPS)
        to_core[rows] = jnp.where(core == 0, last, first)
        to_cross[rows] = jnp.where(core == 0, first, last)


def turn(*pieces):
    return jnp.concatenate(pieces).T


def middle_kernel(packed, middle):
    lats, lon_count = packed.shape
    width = middle.shape[3]
    turned = turn(packed[...], packed[...])

    def column(f, i):
        return jnp.broadcast_to(turned[f * width : (f + 1) * width, i : i + 1], (width, lon_count))

    for i in range(lats):
        spread = column(2 * STEPS, i)
        for step in range(STEPS):
            found = weights(column(step, i), column(STEPS + step, i), spread)
            for at, weight in enumerate(found):
                middle[step, i, at] = weight


def first_kernel(banded, middle, from_core, from_cross, *outs_and_done):
    *outs, done = outs_and_done
    lat, _, core = place()
    lats, width, lon_count = banded.shape
    edge = lats * STEPS
    left = jnp.where(core == 0, from_cross[...], from_core[...])
    right = jnp.where(core == 0, from_core[...], from_cross[...])
    turned = turn(left[edge:], right[edge:])

    def column(f, i):
        low = turned[(f + 1) * width - 8 : (f + 1) * width, i : i + 1]
        high = turned[f * width : f * width + 8, lats + i : lats + i + 1]
        return jnp.broadcast_to(jnp.concatenate([low, high]), (16, lon_count))

    gap = jnp.zeros((8 - STEPS, lon_count), jnp.float32)
    field = []
    for i in range(lats):
        rows = slice(i * STEPS, (i + 1) * STEPS)
        field.append(jnp.concatenate([gap, left[rows], banded[i], right[rows], gap]))
    spread = [column(2 * STEPS, i) for i in range(lats)]
    for step in range(STEPS):
        new = []
        for i in range(lats):
            outer = weights(column(step, i), column(STEPS + step, i), spread[i])
            west, east, south, north, here = (
                jnp.concatenate([w[:8], middle[step, i, at], w[8:]]) for at, w in enumerate(outer)
            )
            value = here * field[i]
            value += west * pltpu.roll(field[i], 1, 0)
            value += east * pltpu.roll(field[i], width + 15, 0)
            if i > 0:
                value += south * field[i - 1]
            if i < lats - 1:
                value += north * field[i + 1]
            new.append(value)
        field = new
    for i in range(lats):
        done[i] = field[i][8 : 8 + width].reshape(done.shape[1:])
    tiles = width // 8
    for target, out in zip([lat] + rows_here(False), outs):
        for slot in range(3):
            i = jnp.clip(target - 1 + slot, 0, lats - 1)
            out[slot * tiles : (slot + 1) * tiles] = done[i]


def assemble_kernel(packed, from_core, from_cross, far, second, relay, ready):
    lat, lon, core = place()
    lats, lon_count = packed.shape
    edge = lats * STEPS
    width = lon_count // lax.axis_size("lon")
    blocks = lon_count // width
    way = 2 * core - 1
    partner = lon ^ 1
    pieces = [
        (packed[...], lon),
        (from_core[edge:], partner),
        (from_cross[edge:], lon + way),
        (far[...], lon + 4),
        (second[...], lon + 2 * way),
        (relay[:lats], partner - way),
        (relay[lats : 2 * lats], partner + 4),
        (relay[2 * lats :], partner - 2 * way),
    ]
    group = lax.broadcasted_iota(jnp.int32, (lats, lon_count), 1) // width
    turned = []
    for piece, at in pieces:
        at = lax.rem(at + blocks, blocks)
        turned.append((pltpu.roll(piece, at * width, 1), group == at))
    fields = []
    for f in range(FIELDS):
        total = None
        for piece, mask in turned:
            back = piece if f == 0 else pltpu.roll(piece, lon_count - f * width, 1)
            part = jnp.where(mask, back, 0.0)
            total = part if total is None else total + part
        fields.append(total)
    for step in range(STEPS):
        west, east, south, north, here = weights(
            fields[step], fields[STEPS + step], fields[2 * STEPS]
        )
        for row in range(lats):
            near = north if row % 2 == 0 else south
            over = north if row == 1 else south
            for at, weight in enumerate((west, east, near, over, here)):
                line = weight[row : row + 1]
                if at == 3 and row in (0, 3):
                    line = jnp.zeros_like(line)
                ready[step, at, lat ^ row] = jnp.broadcast_to(line, (8, lon_count))


def second_kernel(ready, kept, own, *ins_and_rest):
    *ins, out, held, result = ins_and_rest
    lat, _, _ = place()
    lon_count = kept.shape[1]
    for row, block in zip(rows_here(True), ins):
        held[lat ^ row] = block[...]
    values = [own[...]] + [held[slot] for slot in (1, 2, 3)]
    for step, slots in enumerate(((0, 1, 2, 3), (0, 1, 3), (0,))):
        new = list(values)
        for s in slots:
            west, east, near, over, here = (ready[step, at, s][None] for at in range(5))
            value = here * values[s] + near * values[s ^ 1] + over * values[s ^ 3]
            value += west * pltpu.roll(values[s], 1, 2)
            value += east * pltpu.roll(values[s], lon_count - 1, 2)
            new[s] = value
        values = new
    result[...] = values[0].reshape(result.shape)
    for i in range(out.shape[1]):
        slot = i - lat + 1
        inside = (slot >= 0) & (slot <= 2)
        keep = (kept[i : i + 1] > 0.0) & inside
        out[0, i] = jnp.where(keep, result[jnp.clip(slot, 0, 2)], 0.0)


def on_chip(*arrays):
    return [pltpu.with_memory_space_constraint(array, pltpu.VMEM) for array in arrays]


def call(kernel, out_shape, scratch_shapes, *arrays):
    return pl.pallas_call(
        kernel,
        out_shape=out_shape,
        in_specs=[VMEM] * len(arrays),
        out_specs=(VMEM,) * len(out_shape) if isinstance(out_shape, tuple) else VMEM,
        scratch_shapes=scratch_shapes,
    )(*on_chip(*arrays))


def single_row(covariance, winds, diffusivity, cutoff):
    _, lats, width, lon_count = covariance.shape
    count = lax.axis_size("lon")

    def shape(*dims):
        return pltpu.VMEM(dims, jnp.float32)

    edge = shape(lats * STEPS + lats, lon_count)
    wind = shape(lats, lon_count)
    tiles = width // 8
    message = shape(3 * tiles, 8, lon_count)
    to_core, to_cross, packed, banded, kept = pl.pallas_call(
        prepare_kernel,
        out_shape=(edge, edge, wind, shape(lats, width, lon_count), wind),
        in_specs=[pl.BlockSpec(memory_space=pl.ANY)] * 4,
        out_specs=(VMEM,) * 5,
        scratch_shapes=[
            pltpu.SMEM(cutoff.shape, jnp.int32),
            shape(*covariance.shape),
            shape(*winds.shape),
            shape(*diffusivity.shape),
            pltpu.SemaphoreType.DMA((4,)),
        ],
    )(cutoff, covariance, winds, diffusivity)

    lons = range(count)
    pair = [(m, m ^ 1) for m in lons]
    way = [2 * (m % 2) - 1 for m in lons]
    from_cross = lax.ppermute(to_cross, "lon", [((m + way[m]) % count, m) for m in lons])
    from_core = lax.ppermute(to_core, "lon", pair)
    far = lax.ppermute(packed, "lon", [((m + 4) % count, m) for m in lons])
    second = lax.ppermute(packed, "lon", [((m + 2 * way[m]) % count, m) for m in lons])
    middle = call(middle_kernel, shape(STEPS, lats, 5, width, lon_count), [], packed)

    outs = call(
        first_kernel,
        (message,) * (1 + EXCHANGES),
        [shape(lats, tiles, 8, lon_count)],
        banded,
        middle,
        from_core,
        from_cross,
    )
    ins = [outs[0]]
    for at in range(EXCHANGES):
        pairs = list(enumerate(ROUTES[at]))
        ins.append(lax.ppermute(outs[1 + at], ("lat", "lon"), pairs))
    winds_here = jnp.concatenate([from_cross[lats * STEPS :], far, second])
    relay = lax.ppermute(winds_here, "lon", pair)
    ready = call(
        assemble_kernel,
        shape(STEPS, 5, lats, 8, lon_count),
        [],
        packed,
        from_core,
        from_cross,
        far,
        second,
        relay,
    )
    return call(
        second_kernel,
        jax.ShapeDtypeStruct(covariance.shape, jnp.float32),
        [shape(lats, 3 * tiles, 8, lon_count), shape(3, width, lon_count)],
        ready,
        kept,
        *ins,
    )


def per_device(covariance, winds, diffusivity, cutoff):
    fits = lax.axis_size("lat") == 4 and lax.axis_size("lon") == 8
    fits = fits and covariance.shape == (1, 4, 16, 128)
    return (single_row if fits else general)(covariance, winds, diffusivity, cutoff)


def solution(mesh):
    in_specs = (P("lat", None, "lon", None), P(None, None, None, "lon"), P(None, "lon"), P())
    out_specs = P("lat", None, "lon", None)
    return jax.shard_map(
        per_device, mesh=mesh, in_specs=in_specs, out_specs=out_specs, check_vma=False
    )
```

profile of v0, /device:TPU:18, one launch (start us, length us, event | category | flops | bytes accessed | tf_op | source)
XLA Modules:
  0.0 14.8 jit_solution(6598098369343026051)
XLA Ops:
  0.0 0.9 %shard_map.46 = (f32[16,128]{1,0:T(8,128)S(1)}, f32[16,128]{1,0:T(8,128)S(1)}, f32[4,128]{1,0:T(4,128)S(1)}, f32[4,16,128]{2,1,0:T(8,128)S(1)}, f32[4,128]{1,0:T(4,128)S(1)}) custom-call(s32[4]{0:T(128)} %cutoff_in.1, f32[1,4,16,128]{3,2,1,0:T(8,128)} %covariance_in.1, f32[2,3,4,16]{3,2,1,0:T(4,128)} %winds_in.1, f32[4,16]{1,0:T(4,128)} %diffusivity_in.1), custom_call_target="tpu_custom_call" | custom-call | tf_op jit(solution)/shard_map/pallas_call | solution.py:337
  0.9 0.1 collective-permute-start
  0.9 0.6 %collective-permute-start.1 = (f32[16,128]{1,0:T(8,128)S(1)}, f32[16,128]{1,0:T(8,128)S(1)}, u32[]{:S(2)}, u32[]{:S(2)}) collective-permute-start(f32[16,128]{1,0:T(8,128)S(1)} %get-tuple-element.17), channel_id=1, source_target_pairs={{7,0},{2,1},{1,2},{4,3},{3,4},{6,5},{5,6},{0,7},{15,8},{10,9},{9,1... | collective-permute-start | bytes 24584 | tf_op jit(solution)/shard_map/ppermute | solution.py:354
  1.6 2.4 %collective-permute-start.3 = (f32[4,128]{1,0:T(4,128)S(1)}, f32[4,128]{1,0:T(4,128)S(1)}, u32[]{:S(2)}, u32[]{:S(2)}) collective-permute-start(f32[4,128]{1,0:T(4,128)S(1)} %get-tuple-element.15.packed), channel_id=1, source_target_pairs={{6,0},{3,1},{0,2},{5,3},{2,4},{7,5},{4,6},{1,7},{14,8},{11,9},{8,1... | collective-permute-start | bytes 6152 | tf_op jit(solution)/shard_map/ppermute | solution.py:357
  4.0 1.5 %collective-permute-start.2 = (f32[4,128]{1,0:T(4,128)S(1)}, f32[4,128]{1,0:T(4,128)S(1)}, u32[]{:S(2)}, u32[]{:S(2)}) collective-permute-start(f32[4,128]{1,0:T(4,128)S(1)} %get-tuple-element.15.packed), channel_id=1, source_target_pairs={{4,0},{5,1},{6,2},{7,3},{0,4},{1,5},{2,6},{3,7},{12,8},{13,9},{14,... | collective-permute-start | bytes 6152 | tf_op jit(solution)/shard_map/ppermute | solution.py:356
  5.5 0.2 %shard_map.48.middle = f32[3,4,5,16,128]{4,3,2,1,0:T(8,128)S(1)} custom-call(f32[4,128]{1,0:T(4,128)S(1)} %get-tuple-element.15.packed), custom_call_target="tpu_custom_call" | custom-call | tf_op jit(solution)/shard_map/pallas_call | solution.py:317
  5.7 0.0 collective-permute-done.from_core
  5.8 0.0 collective-permute-done.1.from_cross
  5.8 0.3 %shard_map.49 = (f32[6,8,128]{2,1,0:T(8,128)S(1)}, f32[6,8,128]{2,1,0:T(8,128)S(1)}, f32[6,8,128]{2,1,0:T(8,128)S(1)}, f32[6,8,128]{2,1,0:T(8,128)S(1)}, f32[6,8,128]{2,1,0:T(8,128)S(1)}) custom-call(f32[4,16,128]{2,1,0:T(8,128)S(1)} %get-tuple-element.19.banded, f32[3,4,5,16,128]{4,3,2,1,0:T(8,128)S(1)} %shard_map.48.middle, ...), custom_call_target="tpu_custom_call" | custom-call | tf_op jit(solution)/shard_map/pallas_call | solution.py:317
  6.1 1.6 %collective-permute-start.5 = (f32[6,8,128]{2,1,0:T(8,128)S(1)}, f32[6,8,128]{2,1,0:T(8,128)S(1)}, u32[]{:S(2)}, u32[]{:S(2)}) collective-permute-start(f32[6,8,128]{2,1,0:T(8,128)S(1)} %get-tuple-element.21), channel_id=1, source_target_pairs={{0,8},{1,9},{2,10},{3,11},{4,12},{5,13},{6,22},{7,14},{8,16},{9,17... | collective-permute-start | bytes 73736 | tf_op jit(solution)/shard_map/ppermute | solution.py:372
  7.7 0.0 collective-permute-start.6
  7.7 0.8 %collective-permute-start.7 = (f32[6,8,128]{2,1,0:T(8,128)S(1)}, f32[6,8,128]{2,1,0:T(8,128)S(1)}, u32[]{:S(2)}, u32[]{:S(2)}) collective-permute-start(f32[6,8,128]{2,1,0:T(8,128)S(1)} %get-tuple-element.23), channel_id=1, source_target_pairs={{0,24},{1,25},{2,26},{3,27},{4,28},{5,21},{6,30},{7,15},{8,0},{9,1... | collective-permute-start | bytes 73736 | tf_op jit(solution)/shard_map/ppermute | solution.py:372
  8.5 0.0 collective-permute-done.3.second
  8.5 1.2 %collective-permute-start.8 = (f32[6,8,128]{2,1,0:T(8,128)S(1)}, f32[6,8,128]{2,1,0:T(8,128)S(1)}, u32[]{:S(2)}, u32[]{:S(2)}) collective-permute-start(f32[6,8,128]{2,1,0:T(8,128)S(1)} %get-tuple-element.24), channel_id=1, source_target_pairs={{0,16},{1,0},{2,18},{3,2},{4,5},{5,4},{6,7},{7,31},{8,24},{9,1},{1... | collective-permute-start | bytes 73736 | tf_op jit(solution)/shard_map/ppermute | solution.py:372
  9.7 0.0 collective-permute-done.2.far
  9.8 0.1 collective-permute-start.4
  9.8 1.2 %collective-permute-done.4.relay = f32[12,128]{1,0:T(8,128)S(1)} collective-permute-done((f32[12,128]{1,0:T(8,128)S(1)}, f32[12,128]{1,0:T(8,128)S(1)}, u32[]{:S(2)}, u32[]{:S(2)}) %collective-permute-start.4) | collective-permute-done | bytes 6176 | tf_op jit(solution)/shard_map/ppermute | solution.py:374
  11.0 0.2 %shard_map.47.ready = f32[3,5,4,8,128]{4,3,2,1,0:T(8,128)S(1)} custom-call(f32[4,128]{1,0:T(4,128)S(1)} %get-tuple-element.15.packed, f32[16,128]{1,0:T(8,128)S(1)} %collective-permute-done.from_core, f32[16,128]{1,0:T(8,128)S(1)} %collective-permute-done.1.from_cross, f32[4,128]{1,0:T(4,128)S(1)} %collective-permute-done.2.far, ...), custom_call_target="tpu_custom_call" | custom-call | tf_op jit(solution)/shard_map/pallas_call | solution.py:317
  11.2 0.0 collective-permute-done.5.ins_and_rest_0_
  11.2 0.3 %collective-permute-done.6.ins_and_rest_1_ = f32[6,8,128]{2,1,0:T(8,128)S(1)} collective-permute-done((f32[6,8,128]{2,1,0:T(8,128)S(1)}, f32[6,8,128]{2,1,0:T(8,128)S(1)}, u32[]{:S(2)}, u32[]{:S(2)}) %collective-permute-start.6) | collective-permute-done | bytes 24608 | tf_op jit(solution)/shard_map/ppermute | solution.py:372
  11.5 0.0 collective-permute-done.7.ins_and_rest_2_
  11.5 2.4 %collective-permute-done.8.ins_and_rest_3_ = f32[6,8,128]{2,1,0:T(8,128)S(1)} collective-permute-done((f32[6,8,128]{2,1,0:T(8,128)S(1)}, f32[6,8,128]{2,1,0:T(8,128)S(1)}, u32[]{:S(2)}, u32[]{:S(2)}) %collective-permute-start.8) | collective-permute-done | bytes 24608 | tf_op jit(solution)/shard_map/ppermute | solution.py:372
  13.9 0.9 %shard_map.50 = f32[1,4,16,128]{3,2,1,0:T(8,128)} custom-call(f32[3,5,4,8,128]{4,3,2,1,0:T(8,128)S(1)} %shard_map.47.ready, f32[4,128]{1,0:T(4,128)S(1)} %get-tuple-element.18.kept, f32[6,8,128]{2,1,0:T(8,128)S(1)} %get-tuple-element.20.own, f32[6,8,128]{2,1,0:T(8,128)S(1)} %collective-permute-done.5.ins_and_rest_0_, ...), custom_call_target="tpu_custom_call" | custom-call | tf_op jit(solution)/shard_map/pallas_call | solution.py:317
  (2 shorter events, 0.0 us)
Async XLA Ops:
  0.9 4.9 %collective-permute-start = (f32[16,128]{1,0:T(8,128)S(1)}, f32[16,128]{1,0:T(8,128)S(1)}, u32[]{:S(2)}, u32[]{:S(2)}) collective-permute-start(f32[16,128]{1,0:T(8,128)S(1)} %get-tuple-element.16), channel_id=1, source_target_pairs={{0,1},{1,0},{2,3},{3,2},{4,5},{5,4},{6,7},{7,6},{8,9},{9,8},{10,11... | collective-permute-start | bytes 24584 | tf_op jit(solution)/shard_map/ppermute | solution.py:355
  0.9 4.8 %collective-permute-start.1 = (f32[16,128]{1,0:T(8,128)S(1)}, f32[16,128]{1,0:T(8,128)S(1)}, u32[]{:S(2)}, u32[]{:S(2)}) collective-permute-start(f32[16,128]{1,0:T(8,128)S(1)} %get-tuple-element.17), channel_id=1, source_target_pairs={{7,0},{2,1},{1,2},{4,3},{3,4},{6,5},{5,6},{0,7},{15,8},{10,9},{9,1... | collective-permute-start | bytes 24584 | tf_op jit(solution)/shard_map/ppermute | solution.py:354
  1.6 6.9 %collective-permute-start.3 = (f32[4,128]{1,0:T(4,128)S(1)}, f32[4,128]{1,0:T(4,128)S(1)}, u32[]{:S(2)}, u32[]{:S(2)}) collective-permute-start(f32[4,128]{1,0:T(4,128)S(1)} %get-tuple-element.15.packed), channel_id=1, source_target_pairs={{6,0},{3,1},{0,2},{5,3},{2,4},{7,5},{4,6},{1,7},{14,8},{11,9},{8,1... | collective-permute-start | bytes 6152 | tf_op jit(solution)/shard_map/ppermute | solution.py:357
  4.0 5.8 %collective-permute-start.2 = (f32[4,128]{1,0:T(4,128)S(1)}, f32[4,128]{1,0:T(4,128)S(1)}, u32[]{:S(2)}, u32[]{:S(2)}) collective-permute-start(f32[4,128]{1,0:T(4,128)S(1)} %get-tuple-element.15.packed), channel_id=1, source_target_pairs={{4,0},{5,1},{6,2},{7,3},{0,4},{1,5},{2,6},{3,7},{12,8},{13,9},{14,... | collective-permute-start | bytes 6152 | tf_op jit(solution)/shard_map/ppermute | solution.py:356
  6.1 5.1 %collective-permute-start.5 = (f32[6,8,128]{2,1,0:T(8,128)S(1)}, f32[6,8,128]{2,1,0:T(8,128)S(1)}, u32[]{:S(2)}, u32[]{:S(2)}) collective-permute-start(f32[6,8,128]{2,1,0:T(8,128)S(1)} %get-tuple-element.21), channel_id=1, source_target_pairs={{0,8},{1,9},{2,10},{3,11},{4,12},{5,13},{6,22},{7,14},{8,16},{9,17... | collective-permute-start | bytes 73736 | tf_op jit(solution)/shard_map/ppermute | solution.py:372
  7.7 3.8 %collective-permute-start.6 = (f32[6,8,128]{2,1,0:T(8,128)S(1)}, f32[6,8,128]{2,1,0:T(8,128)S(1)}, u32[]{:S(2)}, u32[]{:S(2)}) collective-permute-start(f32[6,8,128]{2,1,0:T(8,128)S(1)} %get-tuple-element.22), channel_id=1, source_target_pairs={{0,3},{1,17},{2,10},{3,19},{4,20},{5,29},{6,14},{7,23},{8,9},{9,25... | collective-permute-start | bytes 73736 | tf_op jit(solution)/shard_map/ppermute | solution.py:372
  7.7 3.8 %collective-permute-start.7 = (f32[6,8,128]{2,1,0:T(8,128)S(1)}, f32[6,8,128]{2,1,0:T(8,128)S(1)}, u32[]{:S(2)}, u32[]{:S(2)}) collective-permute-start(f32[6,8,128]{2,1,0:T(8,128)S(1)} %get-tuple-element.23), channel_id=1, source_target_pairs={{0,24},{1,25},{2,26},{3,27},{4,28},{5,21},{6,30},{7,15},{8,0},{9,1... | collective-permute-start | bytes 73736 | tf_op jit(solution)/shard_map/ppermute | solution.py:372
  8.5 5.4 %collective-permute-start.8 = (f32[6,8,128]{2,1,0:T(8,128)S(1)}, f32[6,8,128]{2,1,0:T(8,128)S(1)}, u32[]{:S(2)}, u32[]{:S(2)}) collective-permute-start(f32[6,8,128]{2,1,0:T(8,128)S(1)} %get-tuple-element.24), channel_id=1, source_target_pairs={{0,16},{1,0},{2,18},{3,2},{4,5},{5,4},{6,7},{7,31},{8,24},{9,1},{1... | collective-permute-start | bytes 73736 | tf_op jit(solution)/shard_map/ppermute | solution.py:372
  9.8 1.2 %collective-permute-start.4 = (f32[12,128]{1,0:T(8,128)S(1)}, f32[12,128]{1,0:T(8,128)S(1)}, u32[]{:S(2)}, u32[]{:S(2)}) collective-permute-start(f32[12,128]{1,0:T(8,128)S(1)} %pad_maximum_fusion), channel_id=1, source_target_pairs={{0,1},{1,0},{2,3},{3,2},{4,5},{5,4},{6,7},{7,6},{8,9},{9,8},{10,11... | collective-permute-start | bytes 18440 | tf_op jit(solution)/shard_map/ppermute | solution.py:374
where the time goes:
time: 15 us; the launch traced here: 14.8 us
  starting transfers between devices  8.35 us (56%)
  waiting for transfers between devices  3.88 us (26%)
  Pallas kernels  2.47 us (16%)
    ppermute x4, starting transfers between devices, single_row(): ins.append(lax.ppermute(outs[1 + at], ('lat', 'lon'), pairs))  3.66 us
    ppermute x4, waiting for transfers between devices, single_row(): ins.append(lax.ppermute(outs[1 + at], ('lat', 'lon'), pairs))  2.71 us
    ppermute x1, starting transfers between devices, single_row(): lax.ppermute(packed, 'lon', [((m + 2 * way[m]) % count, m) for m in lons])  2.39 us
    pallas_call x4, Pallas kernels, call(): pl.pallas_call(kernel, out_shape=out_shape, in_specs=[VMEM] * len(arrays)...  1.61 us
    ppermute x1, starting transfers between devices, single_row(): far = lax.ppermute(packed, 'lon', [((m + 4) % count, m) for m in lons])  1.52 us
    ppermute x1, waiting for transfers between devices, single_row(): relay = lax.ppermute(winds_here, 'lon', pair)  1.16 us
    pallas_call x1, Pallas kernels, single_row(): pl.pallas_call(prepare_kernel, out_shape=(edge, edge, wind, shape(lats, w...  0.86 us
    ppermute x1, starting transfers between devices, single_row(): lax.ppermute(to_cross, 'lon', [((m + way[m]) % count, m) for m in lons])  0.64 us
  transfers between devices with their start and end apart: 9, of which 3 were waited for; matrix products, arithmetic and copies ran while one was open for 0% of the time, Pallas kernels for 5%

commit v1 on v0

--- a/solution.py
+++ b/solution.py
@@ -135,6 +135,7 @@
     covariance,
     winds,
     diffusivity,
+    lines,
     arrived,
 ):
     copies = [
@@ -163,6 +164,17 @@
     rows = pl.ds(lats * STEPS, lats)
     to_core[rows] = packed[...]
     to_cross[rows] = packed[...]
+    lines[...] = jnp.zeros_like(lines)
+    for step in range(STEPS):
+        for kind in range(2):
+            at = (kind * STEPS + step) * lats
+            lines[at : at + lats, :width] = winds[kind, step]
+    lines[2 * STEPS * lats : FIELDS * lats, :width] = diffusivity[...]
+    turned = lines[...].T
+    first, last = turned[:8], turned[width - 8 : width]
+    past = lats * (STEPS + 1)
+    to_core[past:] = jnp.where(core == 0, last, first)
+    to_cross[past:] = jnp.where(core == 0, first, last)
     copies[2].wait()
     copies[3].wait()
     for i in range(lats):
@@ -202,11 +214,10 @@
     edge = lats * STEPS
     left = jnp.where(core == 0, from_cross[...], from_core[...])
     right = jnp.where(core == 0, from_core[...], from_cross[...])
-    turned = turn(left[edge:], right[edge:])
+    past = edge + lats
 
     def column(f, i):
-        low = turned[(f + 1) * width - 8 : (f + 1) * width, i : i + 1]
-        high = turned[f * width : f * width + 8, lats + i : lats + i + 1]
+        low, high = (side[past:, f * lats + i : f * lats + i + 1] for side in (left, right))
         return jnp.broadcast_to(jnp.concatenate([low, high]), (16, lon_count))
 
     gap = jnp.zeros((8 - STEPS, lon_count), jnp.float32)
@@ -250,8 +261,8 @@
     partner = lon ^ 1
     pieces = [
         (packed[...], lon),
-        (from_core[edge:], partner),
-        (from_cross[edge:], lon + way),
+        (from_core[edge : edge + lats], partner),
+        (from_cross[edge : edge + lats], lon + way),
         (far[...], lon + 4),
         (second[...], lon + 2 * way),
         (relay[:lats], partner - way),
@@ -330,7 +341,7 @@
     def shape(*dims):
         return pltpu.VMEM(dims, jnp.float32)
 
-    edge = shape(lats * STEPS + lats, lon_count)
+    edge = shape(lats * (STEPS + 1) + 8, lon_count)
     wind = shape(lats, lon_count)
     tiles = width // 8
     message = shape(3 * tiles, 8, lon_count)
@@ -344,6 +355,7 @@
             shape(*covariance.shape),
             shape(*winds.shape),
             shape(*diffusivity.shape),
+            shape(lon_count, lon_count),
             pltpu.SemaphoreType.DMA((4,)),
         ],
     )(cutoff, covariance, winds, diffusivity)
@@ -370,7 +382,9 @@
     for at in range(EXCHANGES):
         pairs = list(enumerate(ROUTES[at]))
         ins.append(lax.ppermute(outs[1 + at], ("lat", "lon"), pairs))
-    winds_here = jnp.concatenate([from_cross[lats * STEPS :], far, second])
+    winds_here = jnp.concatenate(
+        [from_cross[lats * STEPS : lats * (STEPS + 1)], far, second]
+    )
     relay = lax.ppermute(winds_here, "lon", pair)
     ready = call(
         assemble_kernel,

time: 15 us -> 14.9 us (level)
  transfers between devices with their start and end apart: 9 -> 9, of which waited for: 3 -> 3; matrix products, arithmetic and copies ran while one was open for 0% -> 0% of each run, Pallas kernels for 5% -> 4%
where the time goes in v1:
time: 14.9 us; the launch traced here: 14.7 us
  starting transfers between devices  8.35 us (56%)
  waiting for transfers between devices  3.88 us (26%)
  Pallas kernels  2.35 us (16%)
    ppermute x4, starting transfers between devices, single_row(): ins.append(lax.ppermute(outs[1 + at], ('lat', 'lon'), pairs))  3.66 us
    ppermute x4, waiting for transfers between devices, single_row(): ins.append(lax.ppermute(outs[1 + at], ('lat', 'lon'), pairs))  2.71 us
    ppermute x1, starting transfers between devices, single_row(): lax.ppermute(packed, 'lon', [((m + 2 * way[m]) % count, m) for m in lons])  2.39 us
    ppermute x1, starting transfers between devices, single_row(): far = lax.ppermute(packed, 'lon', [((m + 4) % count, m) for m in lons])  1.52 us
    pallas_call x4, Pallas kernels, call(): pl.pallas_call(kernel, out_shape=out_shape, in_specs=[VMEM] * len(arrays)...  1.49 us
    ppermute x1, waiting for transfers between devices, single_row(): relay = lax.ppermute(winds_here, 'lon', pair)  1.16 us
    pallas_call x1, Pallas kernels, single_row(): pl.pallas_call(prepare_kernel, out_shape=(edge, edge, wind, shape(lats, w...  0.87 us
    ppermute x1, starting transfers between devices, single_row(): lax.ppermute(to_cross, 'lon', [((m + way[m]) % count, m) for m in lons])  0.64 us
  transfers between devices with their start and end apart: 9, of which 3 were waited for; matrix products, arithmetic and copies ran while one was open for 0% of the time, Pallas kernels for 4%

profile of v1, /device:TPU:18, one launch (start us, length us, event | category | flops | bytes accessed | tf_op | source)
XLA Modules:
  0.0 14.7 jit_solution(4240212183745573066)
XLA Ops:
  0.0 0.9 %shard_map.46 = (f32[24,128]{1,0:T(8,128)S(1)}, f32[24,128]{1,0:T(8,128)S(1)}, f32[4,128]{1,0:T(4,128)S(1)}, f32[4,16,128]{2,1,0:T(8,128)S(1)}, f32[4,128]{1,0:T(4,128)S(1)}) custom-call(s32[4]{0:T(128)} %cutoff_in.1, f32[1,4,16,128]{3,2,1,0:T(8,128)} %covariance_in.1, f32[2,3,4,16]{3,2,1,0:T(4,128)} %winds_in.1, f32[4,16]{1,0:T(4,128)} %diffusivity_in.1), custom_call_target="tpu_custom_call" | custom-call | tf_op jit(solution)/shard_map/pallas_call | solution.py:348
  0.9 0.1 collective-permute-start
  1.0 0.6 %collective-permute-start.1 = (f32[24,128]{1,0:T(8,128)S(1)}, f32[24,128]{1,0:T(8,128)S(1)}, u32[]{:S(2)}, u32[]{:S(2)}) collective-permute-start(f32[24,128]{1,0:T(8,128)S(1)} %get-tuple-element.17), channel_id=1, source_target_pairs={{7,0},{2,1},{1,2},{4,3},{3,4},{6,5},{5,6},{0,7},{15,8},{10,9},{9,1... | collective-permute-start | bytes 36872 | tf_op jit(solution)/shard_map/ppermute | solution.py:366
  1.6 2.4 %collective-permute-start.3 = (f32[4,128]{1,0:T(4,128)S(1)}, f32[4,128]{1,0:T(4,128)S(1)}, u32[]{:S(2)}, u32[]{:S(2)}) collective-permute-start(f32[4,128]{1,0:T(4,128)S(1)} %get-tuple-element.15.packed), channel_id=1, source_target_pairs={{6,0},{3,1},{0,2},{5,3},{2,4},{7,5},{4,6},{1,7},{14,8},{11,9},{8,1... | collective-permute-start | bytes 6152 | tf_op jit(solution)/shard_map/ppermute | solution.py:369
  4.0 1.5 %collective-permute-start.2 = (f32[4,128]{1,0:T(4,128)S(1)}, f32[4,128]{1,0:T(4,128)S(1)}, u32[]{:S(2)}, u32[]{:S(2)}) collective-permute-start(f32[4,128]{1,0:T(4,128)S(1)} %get-tuple-element.15.packed), channel_id=1, source_target_pairs={{4,0},{5,1},{6,2},{7,3},{0,4},{1,5},{2,6},{3,7},{12,8},{13,9},{14,... | collective-permute-start | bytes 6152 | tf_op jit(solution)/shard_map/ppermute | solution.py:368
  5.5 0.2 %shard_map.48.middle = f32[3,4,5,16,128]{4,3,2,1,0:T(8,128)S(1)} custom-call(f32[4,128]{1,0:T(4,128)S(1)} %get-tuple-element.15.packed), custom_call_target="tpu_custom_call" | custom-call | tf_op jit(solution)/shard_map/pallas_call | solution.py:328
  5.8 0.0 collective-permute-done.from_core
  5.8 0.0 collective-permute-done.1.from_cross
  5.8 0.2 %shard_map.49 = (f32[6,8,128]{2,1,0:T(8,128)S(1)}, f32[6,8,128]{2,1,0:T(8,128)S(1)}, f32[6,8,128]{2,1,0:T(8,128)S(1)}, f32[6,8,128]{2,1,0:T(8,128)S(1)}, f32[6,8,128]{2,1,0:T(8,128)S(1)}) custom-call(f32[4,16,128]{2,1,0:T(8,128)S(1)} %get-tuple-element.19.banded, f32[3,4,5,16,128]{4,3,2,1,0:T(8,128)S(1)} %shard_map.48.middle, ...), custom_call_target="tpu_custom_call" | custom-call | tf_op jit(solution)/shard_map/pallas_call | solution.py:328
  6.0 1.6 %collective-permute-start.5 = (f32[6,8,128]{2,1,0:T(8,128)S(1)}, f32[6,8,128]{2,1,0:T(8,128)S(1)}, u32[]{:S(2)}, u32[]{:S(2)}) collective-permute-start(f32[6,8,128]{2,1,0:T(8,128)S(1)} %get-tuple-element.21), channel_id=1, source_target_pairs={{0,8},{1,9},{2,10},{3,11},{4,12},{5,13},{6,22},{7,14},{8,16},{9,17... | collective-permute-start | bytes 73736 | tf_op jit(solution)/shard_map/ppermute | solution.py:384
  7.6 0.0 collective-permute-start.6
  7.6 0.8 %collective-permute-start.7 = (f32[6,8,128]{2,1,0:T(8,128)S(1)}, f32[6,8,128]{2,1,0:T(8,128)S(1)}, u32[]{:S(2)}, u32[]{:S(2)}) collective-permute-start(f32[6,8,128]{2,1,0:T(8,128)S(1)} %get-tuple-element.23), channel_id=1, source_target_pairs={{0,24},{1,25},{2,26},{3,27},{4,28},{5,21},{6,30},{7,15},{8,0},{9,1... | collective-permute-start | bytes 73736 | tf_op jit(solution)/shard_map/ppermute | solution.py:384
  8.4 0.0 collective-permute-done.3.second
  8.4 1.2 %collective-permute-start.8 = (f32[6,8,128]{2,1,0:T(8,128)S(1)}, f32[6,8,128]{2,1,0:T(8,128)S(1)}, u32[]{:S(2)}, u32[]{:S(2)}) collective-permute-start(f32[6,8,128]{2,1,0:T(8,128)S(1)} %get-tuple-element.24), channel_id=1, source_target_pairs={{0,16},{1,0},{2,18},{3,2},{4,5},{5,4},{6,7},{7,31},{8,24},{9,1},{1... | collective-permute-start | bytes 73736 | tf_op jit(solution)/shard_map/ppermute | solution.py:384
  9.6 0.0 collective-permute-done.2.far
  9.6 0.1 collective-permute-start.4
  9.7 1.2 %collective-permute-done.4.relay = f32[12,128]{1,0:T(8,128)S(1)} collective-permute-done((f32[12,128]{1,0:T(8,128)S(1)}, f32[12,128]{1,0:T(8,128)S(1)}, u32[]{:S(2)}, u32[]{:S(2)}) %collective-permute-start.4) | collective-permute-done | bytes 6176 | tf_op jit(solution)/shard_map/ppermute | solution.py:388
  10.9 0.2 %shard_map.47.ready = f32[3,5,4,8,128]{4,3,2,1,0:T(8,128)S(1)} custom-call(f32[4,128]{1,0:T(4,128)S(1)} %get-tuple-element.15.packed, f32[24,128]{1,0:T(8,128)S(1)} %collective-permute-done.from_core, f32[24,128]{1,0:T(8,128)S(1)} %collective-permute-done.1.from_cross, f32[4,128]{1,0:T(4,128)S(1)} %collective-permute-done.2.far, ...), custom_call_target="tpu_custom_call" | custom-call | tf_op jit(solution)/shard_map/pallas_call | solution.py:328
  11.1 0.0 collective-permute-done.5.ins_and_rest_0_
  11.1 0.3 %collective-permute-done.6.ins_and_rest_1_ = f32[6,8,128]{2,1,0:T(8,128)S(1)} collective-permute-done((f32[6,8,128]{2,1,0:T(8,128)S(1)}, f32[6,8,128]{2,1,0:T(8,128)S(1)}, u32[]{:S(2)}, u32[]{:S(2)}) %collective-permute-start.6) | collective-permute-done | bytes 24608 | tf_op jit(solution)/shard_map/ppermute | solution.py:384
  11.4 0.0 collective-permute-done.7.ins_and_rest_2_
  11.4 2.4 %collective-permute-done.8.ins_and_rest_3_ = f32[6,8,128]{2,1,0:T(8,128)S(1)} collective-permute-done((f32[6,8,128]{2,1,0:T(8,128)S(1)}, f32[6,8,128]{2,1,0:T(8,128)S(1)}, u32[]{:S(2)}, u32[]{:S(2)}) %collective-permute-start.8) | collective-permute-done | bytes 24608 | tf_op jit(solution)/shard_map/ppermute | solution.py:384
  13.8 0.9 %shard_map.50 = f32[1,4,16,128]{3,2,1,0:T(8,128)} custom-call(f32[3,5,4,8,128]{4,3,2,1,0:T(8,128)S(1)} %shard_map.47.ready, f32[4,128]{1,0:T(4,128)S(1)} %get-tuple-element.18.kept, f32[6,8,128]{2,1,0:T(8,128)S(1)} %get-tuple-element.20.own, f32[6,8,128]{2,1,0:T(8,128)S(1)} %collective-permute-done.5.ins_and_rest_0_, ...), custom_call_target="tpu_custom_call" | custom-call | tf_op jit(solution)/shard_map/pallas_call | solution.py:328
  (2 shorter events, 0.0 us)
Async XLA Ops:
  0.9 4.9 %collective-permute-start = (f32[24,128]{1,0:T(8,128)S(1)}, f32[24,128]{1,0:T(8,128)S(1)}, u32[]{:S(2)}, u32[]{:S(2)}) collective-permute-start(f32[24,128]{1,0:T(8,128)S(1)} %get-tuple-element.16), channel_id=1, source_target_pairs={{0,1},{1,0},{2,3},{3,2},{4,5},{5,4},{6,7},{7,6},{8,9},{9,8},{10,11... | collective-permute-start | bytes 36872 | tf_op jit(solution)/shard_map/ppermute | solution.py:367
  1.0 4.8 %collective-permute-start.1 = (f32[24,128]{1,0:T(8,128)S(1)}, f32[24,128]{1,0:T(8,128)S(1)}, u32[]{:S(2)}, u32[]{:S(2)}) collective-permute-start(f32[24,128]{1,0:T(8,128)S(1)} %get-tuple-element.17), channel_id=1, source_target_pairs={{7,0},{2,1},{1,2},{4,3},{3,4},{6,5},{5,6},{0,7},{15,8},{10,9},{9,1... | collective-permute-start | bytes 36872 | tf_op jit(solution)/shard_map/ppermute | solution.py:366
  1.6 6.8 %collective-permute-start.3 = (f32[4,128]{1,0:T(4,128)S(1)}, f32[4,128]{1,0:T(4,128)S(1)}, u32[]{:S(2)}, u32[]{:S(2)}) collective-permute-start(f32[4,128]{1,0:T(4,128)S(1)} %get-tuple-element.15.packed), channel_id=1, source_target_pairs={{6,0},{3,1},{0,2},{5,3},{2,4},{7,5},{4,6},{1,7},{14,8},{11,9},{8,1... | collective-permute-start | bytes 6152 | tf_op jit(solution)/shard_map/ppermute | solution.py:369
  4.0 5.7 %collective-permute-start.2 = (f32[4,128]{1,0:T(4,128)S(1)}, f32[4,128]{1,0:T(4,128)S(1)}, u32[]{:S(2)}, u32[]{:S(2)}) collective-permute-start(f32[4,128]{1,0:T(4,128)S(1)} %get-tuple-element.15.packed), channel_id=1, source_target_pairs={{4,0},{5,1},{6,2},{7,3},{0,4},{1,5},{2,6},{3,7},{12,8},{13,9},{14,... | collective-permute-start | bytes 6152 | tf_op jit(solution)/shard_map/ppermute | solution.py:368
  6.0 5.1 %collective-permute-start.5 = (f32[6,8,128]{2,1,0:T(8,128)S(1)}, f32[6,8,128]{2,1,0:T(8,128)S(1)}, u32[]{:S(2)}, u32[]{:S(2)}) collective-permute-start(f32[6,8,128]{2,1,0:T(8,128)S(1)} %get-tuple-element.21), channel_id=1, source_target_pairs={{0,8},{1,9},{2,10},{3,11},{4,12},{5,13},{6,22},{7,14},{8,16},{9,17... | collective-permute-start | bytes 73736 | tf_op jit(solution)/shard_map/ppermute | solution.py:384
  7.6 3.8 %collective-permute-start.6 = (f32[6,8,128]{2,1,0:T(8,128)S(1)}, f32[6,8,128]{2,1,0:T(8,128)S(1)}, u32[]{:S(2)}, u32[]{:S(2)}) collective-permute-start(f32[6,8,128]{2,1,0:T(8,128)S(1)} %get-tuple-element.22), channel_id=1, source_target_pairs={{0,3},{1,17},{2,10},{3,19},{4,20},{5,29},{6,14},{7,23},{8,9},{9,25... | collective-permute-start | bytes 73736 | tf_op jit(solution)/shard_map/ppermute | solution.py:384
  7.6 3.8 %collective-permute-start.7 = (f32[6,8,128]{2,1,0:T(8,128)S(1)}, f32[6,8,128]{2,1,0:T(8,128)S(1)}, u32[]{:S(2)}, u32[]{:S(2)}) collective-permute-start(f32[6,8,128]{2,1,0:T(8,128)S(1)} %get-tuple-element.23), channel_id=1, source_target_pairs={{0,24},{1,25},{2,26},{3,27},{4,28},{5,21},{6,30},{7,15},{8,0},{9,1... | collective-permute-start | bytes 73736 | tf_op jit(solution)/shard_map/ppermute | solution.py:384
  8.4 5.4 %collective-permute-start.8 = (f32[6,8,128]{2,1,0:T(8,128)S(1)}, f32[6,8,128]{2,1,0:T(8,128)S(1)}, u32[]{:S(2)}, u32[]{:S(2)}) collective-permute-start(f32[6,8,128]{2,1,0:T(8,128)S(1)} %get-tuple-element.24), channel_id=1, source_target_pairs={{0,16},{1,0},{2,18},{3,2},{4,5},{5,4},{6,7},{7,31},{8,24},{9,1},{1... | collective-permute-start | bytes 73736 | tf_op jit(solution)/shard_map/ppermute | solution.py:384
  9.6 1.2 %collective-permute-start.4 = (f32[12,128]{1,0:T(8,128)S(1)}, f32[12,128]{1,0:T(8,128)S(1)}, u32[]{:S(2)}, u32[]{:S(2)}) collective-permute-start(f32[12,128]{1,0:T(8,128)S(1)} %pad_maximum_fusion), channel_id=1, source_target_pairs={{0,1},{1,0},{2,3},{3,2},{4,5},{5,4},{6,7},{7,6},{8,9},{9,8},{10,11... | collective-permute-start | bytes 18440 | tf_op jit(solution)/shard_map/ppermute | solution.py:388

commit v2 on v1

--- a/solution.py
+++ b/solution.py
@@ -131,6 +131,7 @@
     packed,
     banded,
     kept,
+    upright,
     cutoff,
     covariance,
     winds,
@@ -172,6 +173,7 @@
     lines[2 * STEPS * lats : FIELDS * lats, :width] = diffusivity[...]
     turned = lines[...].T
     first, last = turned[:8], turned[width - 8 : width]
+    upright[...] = turned[:width]
     past = lats * (STEPS + 1)
     to_core[past:] = jnp.where(core == 0, last, first)
     to_cross[past:] = jnp.where(core == 0, first, last)
@@ -187,17 +189,13 @@
         to_cross[rows] = jnp.where(core == 0, first, last)
 
 
-def turn(*pieces):
-    return jnp.concatenate(pieces).T
-
-
-def middle_kernel(packed, middle):
-    lats, lon_count = packed.shape
-    width = middle.shape[3]
-    turned = turn(packed[...], packed[...])
+def middle_kernel(upright, middle):
+    width, lon_count = upright.shape
+    lats = middle.shape[1]
 
     def column(f, i):
-        return jnp.broadcast_to(turned[f * width : (f + 1) * width, i : i + 1], (width, lon_count))
+        at = f * lats + i
+        return jnp.broadcast_to(upright[:, at : at + 1], (width, lon_count))
 
     for i in range(lats):
         spread = column(2 * STEPS, i)
@@ -345,11 +343,11 @@
     wind = shape(lats, lon_count)
     tiles = width // 8
     message = shape(3 * tiles, 8, lon_count)
-    to_core, to_cross, packed, banded, kept = pl.pallas_call(
+    to_core, to_cross, packed, banded, kept, upright = pl.pallas_call(
         prepare_kernel,
-        out_shape=(edge, edge, wind, shape(lats, width, lon_count), wind),
+        out_shape=(edge, edge, wind, shape(lats, width, lon_count), wind, shape(width, lon_count)),
         in_specs=[pl.BlockSpec(memory_space=pl.ANY)] * 4,
-        out_specs=(VMEM,) * 5,
+        out_specs=(VMEM,) * 6,
         scratch_shapes=[
             pltpu.SMEM(cutoff.shape, jnp.int32),
             shape(*covariance.shape),
@@ -367,7 +365,7 @@
     from_core = lax.ppermute(to_core, "lon", pair)
     far = lax.ppermute(packed, "lon", [((m + 4) % count, m) for m in lons])
     second = lax.ppermute(packed, "lon", [((m + 2 * way[m]) % count, m) for m in lons])
-    middle = call(middle_kernel, shape(STEPS, lats, 5, width, lon_count), [], packed)
+    middle = call(middle_kernel, shape(STEPS, lats, 5, width, lon_count), [], upright)
 
     outs = call(
         first_kernel,

time: 14.9 us -> 14.8 us (level)
  the two profiles are of different devices: /device:TPU:18 before, /device:TPU:0 now
where the time goes in v2:
time: 14.8 us; the launch traced here: 14.5 us
  starting transfers between devices  10.8 us (73%)
  Pallas kernels  2.26 us (15%)
  waiting for transfers between devices  1.43 us (10%)
    ppermute x4, starting transfers between devices, single_row(): ins.append(lax.ppermute(outs[1 + at], ('lat', 'lon'), pairs))  5.48 us
    ppermute x1, starting transfers between devices, single_row(): lax.ppermute(to_cross, 'lon', [((m + way[m]) % count, m) for m in lons])  3.54 us
    pallas_call x4, Pallas kernels, call(): pl.pallas_call(kernel, out_shape=out_shape, in_specs=[VMEM] * len(arrays)...  1.39 us
    ppermute x1, waiting for transfers between devices, single_row(): relay = lax.ppermute(winds_here, 'lon', pair)  1.16 us
    ppermute x1, starting transfers between devices, single_row(): far = lax.ppermute(packed, 'lon', [((m + 4) % count, m) for m in lons])  1.1 us
    pallas_call x1, Pallas kernels, single_row(): pl.pallas_call(prepare_kernel, out_shape=(edge, edge, wind, shape(lats, w...  0.87 us
    ppermute x1, starting transfers between devices, single_row(): from_core = lax.ppermute(to_core, 'lon', pair)  0.56 us
  transfers between devices with their start and end apart: 9, of which 3 were waited for; matrix products, arithmetic and copies ran while one was open for 0% of the time, Pallas kernels for 4%

profile of v2, /device:TPU:0, one launch (start us, length us, event | category | flops | bytes accessed | tf_op | source)
XLA Modules:
  0.0 14.5 jit_solution(3901320341392438231)
XLA Ops:
  0.0 0.9 %shard_map.46 = (f32[24,128]{1,0:T(8,128)S(1)}, f32[24,128]{1,0:T(8,128)S(1)}, f32[4,128]{1,0:T(4,128)S(1)}, f32[4,16,128]{2,1,0:T(8,128)S(1)}, f32[4,128]{1,0:T(4,128)S(1)}, /*index=5*/f32[16,128]{1,0:T(8,128)S(1)}) custom-call(s32[4]{0:T(128)} %cutoff_in.1, f32[1,4,16,128]{3,2,1,0:T(8,128)} %covariance_in.1, f32[2,3,4,16]{3,2,1,0:T(4,128)} %winds_in.1, ...), custom_call_target="tpu_custom_call" | custom-call | tf_op jit(solution)/shard_map/pallas_call | solution.py:346
  0.9 0.6 %collective-permute-start = (f32[24,128]{1,0:T(8,128)S(1)}, f32[24,128]{1,0:T(8,128)S(1)}, u32[]{:S(2)}, u32[]{:S(2)}) collective-permute-start(f32[24,128]{1,0:T(8,128)S(1)} %get-tuple-element.17), channel_id=1, source_target_pairs={{0,1},{1,0},{2,3},{3,2},{4,5},{5,4},{6,7},{7,6},{8,9},{9,8},{10,11... | collective-permute-start | bytes 36872 | tf_op jit(solution)/shard_map/ppermute | solution.py:365
  1.4 3.5 %collective-permute-start.1 = (f32[24,128]{1,0:T(8,128)S(1)}, f32[24,128]{1,0:T(8,128)S(1)}, u32[]{:S(2)}, u32[]{:S(2)}) collective-permute-start(f32[24,128]{1,0:T(8,128)S(1)} %get-tuple-element.18), channel_id=1, source_target_pairs={{7,0},{2,1},{1,2},{4,3},{3,4},{6,5},{5,6},{0,7},{15,8},{10,9},{9,1... | collective-permute-start | bytes 36872 | tf_op jit(solution)/shard_map/ppermute | solution.py:364
  5.0 0.0 collective-permute-start.3
  5.0 1.1 %collective-permute-start.2 = (f32[4,128]{1,0:T(4,128)S(1)}, f32[4,128]{1,0:T(4,128)S(1)}, u32[]{:S(2)}, u32[]{:S(2)}) collective-permute-start(f32[4,128]{1,0:T(4,128)S(1)} %get-tuple-element.16.packed), channel_id=1, source_target_pairs={{4,0},{5,1},{6,2},{7,3},{0,4},{1,5},{2,6},{3,7},{12,8},{13,9},{14,... | collective-permute-start | bytes 6152 | tf_op jit(solution)/shard_map/ppermute | solution.py:366
  6.1 0.2 %shard_map.48.middle = f32[3,4,5,16,128]{4,3,2,1,0:T(8,128)S(1)} custom-call(f32[16,128]{1,0:T(8,128)S(1)} %get-tuple-element.21.upright), custom_call_target="tpu_custom_call" | custom-call | tf_op jit(solution)/shard_map/pallas_call | solution.py:326
  6.2 0.0 collective-permute-done.from_core
  6.3 0.1 collective-permute-done.1.from_cross
  6.4 0.2 %shard_map.49 = (f32[6,8,128]{2,1,0:T(8,128)S(1)}, f32[6,8,128]{2,1,0:T(8,128)S(1)}, f32[6,8,128]{2,1,0:T(8,128)S(1)}, f32[6,8,128]{2,1,0:T(8,128)S(1)}, f32[6,8,128]{2,1,0:T(8,128)S(1)}) custom-call(f32[4,16,128]{2,1,0:T(8,128)S(1)} %get-tuple-element.20.banded, f32[3,4,5,16,128]{4,3,2,1,0:T(8,128)S(1)} %shard_map.48.middle, ...), custom_call_target="tpu_custom_call" | custom-call | tf_op jit(solution)/shard_map/pallas_call | solution.py:326
  6.6 1.8 %collective-permute-start.5 = (f32[6,8,128]{2,1,0:T(8,128)S(1)}, f32[6,8,128]{2,1,0:T(8,128)S(1)}, u32[]{:S(2)}, u32[]{:S(2)}) collective-permute-start(f32[6,8,128]{2,1,0:T(8,128)S(1)} %get-tuple-element.23), channel_id=1, source_target_pairs={{0,8},{1,9},{2,10},{3,11},{4,12},{5,13},{6,22},{7,14},{8,16},{9,17... | collective-permute-start | bytes 73736 | tf_op jit(solution)/shard_map/ppermute | solution.py:382
  8.3 1.2 %collective-permute-start.6 = (f32[6,8,128]{2,1,0:T(8,128)S(1)}, f32[6,8,128]{2,1,0:T(8,128)S(1)}, u32[]{:S(2)}, u32[]{:S(2)}) collective-permute-start(f32[6,8,128]{2,1,0:T(8,128)S(1)} %get-tuple-element.24), channel_id=1, source_target_pairs={{0,3},{1,17},{2,10},{3,19},{4,20},{5,29},{6,14},{7,23},{8,9},{9,25... | collective-permute-start | bytes 73736 | tf_op jit(solution)/shard_map/ppermute | solution.py:382
  9.6 1.7 %collective-permute-start.7 = (f32[6,8,128]{2,1,0:T(8,128)S(1)}, f32[6,8,128]{2,1,0:T(8,128)S(1)}, u32[]{:S(2)}, u32[]{:S(2)}) collective-permute-start(f32[6,8,128]{2,1,0:T(8,128)S(1)} %get-tuple-element.25), channel_id=1, source_target_pairs={{0,24},{1,25},{2,26},{3,27},{4,28},{5,21},{6,30},{7,15},{8,0},{9,1... | collective-permute-start | bytes 73736 | tf_op jit(solution)/shard_map/ppermute | solution.py:382
  11.3 0.0 collective-permute-done.3.second
  11.3 0.8 %collective-permute-start.8 = (f32[6,8,128]{2,1,0:T(8,128)S(1)}, f32[6,8,128]{2,1,0:T(8,128)S(1)}, u32[]{:S(2)}, u32[]{:S(2)}) collective-permute-start(f32[6,8,128]{2,1,0:T(8,128)S(1)} %get-tuple-element.26), channel_id=1, source_target_pairs={{0,16},{1,0},{2,18},{3,2},{4,5},{5,4},{6,7},{7,31},{8,24},{9,1},{1... | collective-permute-start | bytes 73736 | tf_op jit(solution)/shard_map/ppermute | solution.py:382
  12.1 0.0 collective-permute-done.2.far
  12.1 0.1 collective-permute-start.4
  12.1 1.2 %collective-permute-done.4.relay = f32[12,128]{1,0:T(8,128)S(1)} collective-permute-done((f32[12,128]{1,0:T(8,128)S(1)}, f32[12,128]{1,0:T(8,128)S(1)}, u32[]{:S(2)}, u32[]{:S(2)}) %collective-permute-start.4) | collective-permute-done | bytes 6176 | tf_op jit(solution)/shard_map/ppermute | solution.py:386
  13.3 0.2 %shard_map.47.ready = f32[3,5,4,8,128]{4,3,2,1,0:T(8,128)S(1)} custom-call(f32[4,128]{1,0:T(4,128)S(1)} %get-tuple-element.16.packed, f32[24,128]{1,0:T(8,128)S(1)} %collective-permute-done.from_core, f32[24,128]{1,0:T(8,128)S(1)} %collective-permute-done.1.from_cross, f32[4,128]{1,0:T(4,128)S(1)} %collective-permute-done.2.far, ...), custom_call_target="tpu_custom_call" | custom-call | tf_op jit(solution)/shard_map/pallas_call | solution.py:326
  13.5 0.0 collective-permute-done.5.ins_and_rest_0_
  13.5 0.0 collective-permute-done.6.ins_and_rest_1_
  13.5 0.1 collective-permute-done.7.ins_and_rest_2_
  13.7 0.0 collective-permute-done.8.ins_and_rest_3_
  13.7 0.9 %shard_map.50 = f32[1,4,16,128]{3,2,1,0:T(8,128)} custom-call(f32[3,5,4,8,128]{4,3,2,1,0:T(8,128)S(1)} %shard_map.47.ready, f32[4,128]{1,0:T(4,128)S(1)} %get-tuple-element.19.kept, f32[6,8,128]{2,1,0:T(8,128)S(1)} %get-tuple-element.22.own, f32[6,8,128]{2,1,0:T(8,128)S(1)} %collective-permute-done.5.ins_and_rest_0_, ...), custom_call_target="tpu_custom_call" | custom-call | tf_op jit(solution)/shard_map/pallas_call | solution.py:326
  (2 shorter events, 0.0 us)
Async XLA Ops:
  0.9 5.4 %collective-permute-start = (f32[24,128]{1,0:T(8,128)S(1)}, f32[24,128]{1,0:T(8,128)S(1)}, u32[]{:S(2)}, u32[]{:S(2)}) collective-permute-start(f32[24,128]{1,0:T(8,128)S(1)} %get-tuple-element.17), channel_id=1, source_target_pairs={{0,1},{1,0},{2,3},{3,2},{4,5},{5,4},{6,7},{7,6},{8,9},{9,8},{10,11... | collective-permute-start | bytes 36872 | tf_op jit(solution)/shard_map/ppermute | solution.py:365
  1.4 5.0 %collective-permute-start.1 = (f32[24,128]{1,0:T(8,128)S(1)}, f32[24,128]{1,0:T(8,128)S(1)}, u32[]{:S(2)}, u32[]{:S(2)}) collective-permute-start(f32[24,128]{1,0:T(8,128)S(1)} %get-tuple-element.18), channel_id=1, source_target_pairs={{7,0},{2,1},{1,2},{4,3},{3,4},{6,5},{5,6},{0,7},{15,8},{10,9},{9,1... | collective-permute-start | bytes 36872 | tf_op jit(solution)/shard_map/ppermute | solution.py:364
  5.0 6.3 %collective-permute-start.3 = (f32[4,128]{1,0:T(4,128)S(1)}, f32[4,128]{1,0:T(4,128)S(1)}, u32[]{:S(2)}, u32[]{:S(2)}) collective-permute-start(f32[4,128]{1,0:T(4,128)S(1)} %get-tuple-element.16.packed), channel_id=1, source_target_pairs={{6,0},{3,1},{0,2},{5,3},{2,4},{7,5},{4,6},{1,7},{14,8},{11,9},{8,1... | collective-permute-start | bytes 6152 | tf_op jit(solution)/shard_map/ppermute | solution.py:367
  5.0 7.1 %collective-permute-start.2 = (f32[4,128]{1,0:T(4,128)S(1)}, f32[4,128]{1,0:T(4,128)S(1)}, u32[]{:S(2)}, u32[]{:S(2)}) collective-permute-start(f32[4,128]{1,0:T(4,128)S(1)} %get-tuple-element.16.packed), channel_id=1, source_target_pairs={{4,0},{5,1},{6,2},{7,3},{0,4},{1,5},{2,6},{3,7},{12,8},{13,9},{14,... | collective-permute-start | bytes 6152 | tf_op jit(solution)/shard_map/ppermute | solution.py:366
  6.6 7.0 %collective-permute-start.5 = (f32[6,8,128]{2,1,0:T(8,128)S(1)}, f32[6,8,128]{2,1,0:T(8,128)S(1)}, u32[]{:S(2)}, u32[]{:S(2)}) collective-permute-start(f32[6,8,128]{2,1,0:T(8,128)S(1)} %get-tuple-element.23), channel_id=1, source_target_pairs={{0,8},{1,9},{2,10},{3,11},{4,12},{5,13},{6,22},{7,14},{8,16},{9,17... | collective-permute-start | bytes 73736 | tf_op jit(solution)/shard_map/ppermute | solution.py:382
  8.3 5.2 %collective-permute-start.6 = (f32[6,8,128]{2,1,0:T(8,128)S(1)}, f32[6,8,128]{2,1,0:T(8,128)S(1)}, u32[]{:S(2)}, u32[]{:S(2)}) collective-permute-start(f32[6,8,128]{2,1,0:T(8,128)S(1)} %get-tuple-element.24), channel_id=1, source_target_pairs={{0,3},{1,17},{2,10},{3,19},{4,20},{5,29},{6,14},{7,23},{8,9},{9,25... | collective-permute-start | bytes 73736 | tf_op jit(solution)/shard_map/ppermute | solution.py:382
  9.6 4.1 %collective-permute-start.7 = (f32[6,8,128]{2,1,0:T(8,128)S(1)}, f32[6,8,128]{2,1,0:T(8,128)S(1)}, u32[]{:S(2)}, u32[]{:S(2)}) collective-permute-start(f32[6,8,128]{2,1,0:T(8,128)S(1)} %get-tuple-element.25), channel_id=1, source_target_pairs={{0,24},{1,25},{2,26},{3,27},{4,28},{5,21},{6,30},{7,15},{8,0},{9,1... | collective-permute-start | bytes 73736 | tf_op jit(solution)/shard_map/ppermute | solution.py:382
  11.3 2.4 %collective-permute-start.8 = (f32[6,8,128]{2,1,0:T(8,128)S(1)}, f32[6,8,128]{2,1,0:T(8,128)S(1)}, u32[]{:S(2)}, u32[]{:S(2)}) collective-permute-start(f32[6,8,128]{2,1,0:T(8,128)S(1)} %get-tuple-element.26), channel_id=1, source_target_pairs={{0,16},{1,0},{2,18},{3,2},{4,5},{5,4},{6,7},{7,31},{8,24},{9,1},{1... | collective-permute-start | bytes 73736 | tf_op jit(solution)/shard_map/ppermute | solution.py:382
  12.1 1.2 %collective-permute-start.4 = (f32[12,128]{1,0:T(8,128)S(1)}, f32[12,128]{1,0:T(8,128)S(1)}, u32[]{:S(2)}, u32[]{:S(2)}) collective-permute-start(f32[12,128]{1,0:T(8,128)S(1)} %pad_maximum_fusion), channel_id=1, source_target_pairs={{0,1},{1,0},{2,3},{3,2},{4,5},{5,4},{6,7},{7,6},{8,9},{9,8},{10,11... | collective-permute-start | bytes 18440 | tf_op jit(solution)/shard_map/ppermute | solution.py:386
